TPU v7x, 256 devices: a whole 4x4x8 slice. The times are simulated.
256 devices in a mesh: dp: 4 (over x), expert: 4 (over y), tensor: 16 (over z, core).
Axes of the slice: x: 4, y: 4, z: 8, core: 2. Of those that a mesh axis runs over, the one named last changes fastest.
Arguments:
- tokens: bfloat16 [2048, 4096], P('expert', 'dp'), may hold values from -6 to 6
- labels: int32 [2048, 1], P('expert'), may hold values from 0 to 7; in each aligned block of 512 rows (0 to 511, 512 to 1023, ...) at most 96 rows name the same one
- grad_out: bfloat16 [2048, 4096], P('expert', 'dp'), may hold values from -1.5 to 1.5
- w_gate: bfloat16 [8, 4096, 7168], P('expert', 'dp', 'tensor'), may hold values from -0.09375 to 0.09375
- w_up: bfloat16 [8, 4096, 7168], P('expert', 'dp', 'tensor'), may hold values from -0.09375 to 0.09375
- w_down: bfloat16 [8, 7168, 4096], P('expert', 'tensor', 'dp'), may hold values from -0.0625 to 0.0625
Outputs:
- mixed: bfloat16 [2048, 4096], P('expert', 'dp')
- grad_tokens: bfloat16 [2048, 4096], P('expert', 'dp')
- grad_gate: bfloat16 [8, 4096, 7168], P('expert', 'dp', 'tensor')
- grad_up: bfloat16 [8, 4096, 7168], P('expert', 'dp', 'tensor')
- grad_down: bfloat16 [8, 7168, 4096], P('expert', 'tensor', 'dp')
Inputs may be any that keep to these rules, and one draw needn't show every extreme that they name: `labels`: in each aligned block of 512 rows (the rows of one index of expert) no domain appears more than 96 times; some domain appears exactly 96 times in some block. Every domain appears somewhere.
All inputs are finite; a program needn't handle non-finite values.
Results may differ from a plain program's by a relative error of at most 0.005.
Values may be sent and summed in bfloat16 or wider, within the bound.
A program may use at most 128 MiB of HBM per device.

v0:
```python
import jax
import jax.numpy as jnp
from jax import lax
from jax.sharding import PartitionSpec as P

MOST = 96


def split_up(shard, dim, count):
    dims = shard.shape
    tiles = shard.reshape(*dims[:dim], count, dims[dim] // count, *dims[dim + 1 :])
    return jnp.moveaxis(tiles, dim, 0)


def summed_on_arrival(shard, axis, dim):
    count = lax.axis_size(axis)
    tiles = lax.all_to_all(split_up(shard, dim, count), axis, 0, 0, tiled=True)
    return jnp.sum(tiles, axis=0)


def laid_out(tiles, dim):
    dims = list(tiles.shape[1:])
    dims[dim] *= tiles.shape[0]
    return jnp.moveaxis(tiles, 0, dim).reshape(dims)


def sent_to_all(shard, axis):
    count = lax.axis_size(axis)
    return lax.all_to_all(
        jnp.broadcast_to(shard[None], (count, *shard.shape)), axis, 0, 0, tiled=True
    )


def gather_directly(shard, axis, dim):
    return laid_out(sent_to_all(shard, axis), dim)


def body(tokens, labels, grad_out, w_gate, w_up, w_down):
    local_experts = w_gate.shape[0]
    groups = lax.axis_size("expert")
    experts = local_experts * groups
    feat_width = tokens.shape[1]
    hidden_width = w_gate.shape[2]
    domain = labels[:, 0]
    onehot = (domain[:, None] == jnp.arange(experts, dtype=jnp.int32)[None, :]).astype(jnp.int32)
    before = jnp.cumsum(onehot, axis=0) - onehot
    rank_in = jnp.sum(before * onehot, axis=1)
    slot_of = rank_in * experts + domain
    positions = jnp.arange(experts * MOST, dtype=jnp.int32)
    to_slots = (positions[:, None] == slot_of[None, :]).astype(jnp.bfloat16)
    from_slots = (slot_of[:, None] == positions[None, :]).astype(jnp.bfloat16)
    payload = jnp.concatenate([tokens, grad_out], axis=1)
    packed = jnp.dot(to_slots, payload, preferred_element_type=jnp.float32).astype(jnp.bfloat16)
    packed = packed.reshape(MOST, groups, local_experts, 2 * feat_width)
    arrived = lax.all_to_all(packed, "expert", split_axis=1, concat_axis=1, tiled=True)
    inputs = arrived[..., :feat_width]
    grad_rows = arrived[..., feat_width:]
    gate_part = jnp.einsum("msjd,jdf->msjf", inputs, w_gate, preferred_element_type=jnp.float32)
    up_part = jnp.einsum("msjd,jdf->msjf", inputs, w_up, preferred_element_type=jnp.float32)
    back_part = jnp.einsum("msjd,jfd->msjf", grad_rows, w_down, preferred_element_type=jnp.float32)
    scattered = summed_on_arrival(
        jnp.concatenate([gate_part, up_part, back_part], axis=-1), "dp", 0
    )
    gate_sum = scattered[..., :hidden_width]
    up_sum = scattered[..., hidden_width : 2 * hidden_width]
    back_sum = scattered[..., 2 * hidden_width :]
    sigmoid_gate = jax.nn.sigmoid(gate_sum)
    active = gate_sum * sigmoid_gate
    hidden_act = (active * up_sum).astype(jnp.bfloat16)
    d_gate = (back_sum * up_sum * (sigmoid_gate * (1.0 + gate_sum * (1.0 - sigmoid_gate)))).astype(
        jnp.bfloat16
    )
    d_up = (back_sum * active).astype(jnp.bfloat16)
    local_acts = jnp.concatenate([hidden_act, d_gate, d_up], axis=-1)
    act_rows = gather_directly(local_acts, "dp", 0)
    inputs = arrived[..., :feat_width]
    grad_rows = arrived[..., feat_width:]
    act_piece = act_rows[..., :hidden_width]
    gate_piece = act_rows[..., hidden_width : 2 * hidden_width]
    up_piece = act_rows[..., 2 * hidden_width :]
    forward = jnp.einsum("msjf,jfd->msjd", act_piece, w_down, preferred_element_type=jnp.float32)
    backward = jnp.einsum("msjf,jdf->msjd", gate_piece, w_gate, preferred_element_type=jnp.float32)
    backward = backward + jnp.einsum(
        "msjf,jdf->msjd", up_piece, w_up, preferred_element_type=jnp.float32
    )
    rows_out = jnp.concatenate([forward, backward], axis=-1)
    down_acc = jnp.einsum(
        "msjf,msjd->jfd", act_piece, grad_rows, preferred_element_type=jnp.float32
    )
    gate_acc = jnp.einsum("msjd,msjf->jdf", inputs, gate_piece, preferred_element_type=jnp.float32)
    up_acc = jnp.einsum("msjd,msjf->jdf", inputs, up_piece, preferred_element_type=jnp.float32)
    rows_out, down_acc, gate_acc, up_acc = (rows_out, down_acc, gate_acc, up_acc)
    summed = lax.psum(rows_out, "tensor").astype(jnp.bfloat16)
    home_rows = lax.all_to_all(summed, "expert", split_axis=1, concat_axis=1, tiled=True)
    home_flat = home_rows.reshape(experts * MOST, 2 * feat_width)
    result = jnp.dot(from_slots, home_flat, preferred_element_type=jnp.float32).astype(jnp.bfloat16)
    mixed_rows = result[:, :feat_width]
    grad_rows_home = result[:, feat_width:]
    return (
        mixed_rows,
        grad_rows_home,
        gate_acc.astype(jnp.bfloat16),
        up_acc.astype(jnp.bfloat16),
        down_acc.astype(jnp.bfloat16),
    )


def solution(mesh):
    in_specs = (
        P("expert", "dp"),
        P("expert", None),
        P("expert", "dp"),
        P("expert", "dp", "tensor"),
        P("expert", "dp", "tensor"),
        P("expert", "tensor", "dp"),
    )
    out_specs = (
        P("expert", "dp"),
        P("expert", "dp"),
        P("expert", "dp", "tensor"),
        P("expert", "dp", "tensor"),
        P("expert", "tensor", "dp"),
    )
    return jax.shard_map(body, mesh=mesh, in_specs=in_specs, out_specs=out_specs, check_vma=False)
```

profile of v0, /device:TPU:1, one launch (start us, length us, event | category | flops | bytes accessed | tf_op | source)
XLA Modules:
  0.0 310.1 jit_solution(4098771300753129801)
XLA Ops:
  0.6 0.0 copy-start
  0.6 0.8 fusion.39
  1.5 1.1 reduce-window.6
  2.6 0.2 slice_reduce_fusion
  2.9 0.8 fusion.38
  3.6 0.7 broadcast_multiply_fusion
  4.3 5.0 %convolution_convert_fusion = bf16[768,2048]{1,0:T(8,128)(2,1)} fusion(bf16[512,1024]{1,0:T(8,128)(2,1)} %param.8, bf16[512,1024]{1,0:T(8,128)(2,1)} %param.6, s32[512]{0:T(512)S(1)} %get-tuple-element.13), kind=kOutput, calls=%fused_computation.4 | convolution fusion | flops 1616773120 | bytes 5244928 | tf_op jit(solution)/shard_map/dot_general | solution.py:53
  9.3 6.0 %reshape.57 = bf16[96,4,2,2048]{3,2,1,0:T(2,128)(2,1)} reshape(bf16[768,2048]{1,0:T(8,128)(2,1)} %convolution_convert_fusion) | data formatting | bytes 6291456 | tf_op jit(solution)/shard_map/reshape | solution.py:54
  15.3 3.6 %copy.14 = bf16[96,4,2,2048]{3,0,2,1:T(8,128)(2,1)S(1)} copy(bf16[96,4,2,2048]{3,2,1,0:T(2,128)(2,1)} %reshape.57) | data formatting | bytes 6291456 | tf_op jit(solution)/shard_map/reshape | solution.py:54
  18.9 41.5 %all_to_all.20 = bf16[96,4,2,2048]{3,0,2,1:T(8,128)(2,1)S(1)} all-to-all(bf16[96,4,2,2048]{3,0,2,1:T(8,128)(2,1)S(1)} %copy.14), channel_id=1, replica_groups=mesh['dp'=4,'expert'=4,'tensor'=16] {'expert'}, dimensions={1} | all-to-all | bytes 6291456 | tf_op jit(solution)/shard_map/all_to_all | solution.py:55
  60.4 0.4 fusion.42
  60.9 0.0 copy-start.8
  60.9 0.0 copy-start.10
  60.9 0.0 copy-done
  60.9 0.0 copy-start.6
  60.9 1.0 fusion.13
  62.0 0.0 copy-done.8
  62.0 1.5 copy-done.6
  63.5 2.1 fusion.16
  65.7 2.1 fusion.19
  67.8 5.5 %concatenate.13 = f32[96,4,2,1344]{3,0,1,2:T(8,128)} concatenate(f32[96,4,2,448]{3,0,1,2:T(8,128)S(1)} %fusion.13, f32[96,4,2,448]{3,0,1,2:T(8,128)} %fusion.16, f32[96,4,2,448]{3,0,1,2:T(8,128)} %fusion.19), dimensions={3} | concatenate | bytes 8257536 | tf_op jit(solution)/shard_map/concatenate | solution.py:62
  73.4 2.6 copy.17
  75.9 51.8 %all_to_all.21 = f32[4,24,4,2,1344]{4,1,2,3,0:T(8,128)} all-to-all(f32[4,24,4,2,1344]{4,1,2,3,0:T(8,128)S(1)} %copy.17), channel_id=1, replica_groups=mesh['dp'=4,'expert'=4,'tensor'=16] {'dp'}, dimensions={0} | all-to-all | bytes 8257536 | tf_op jit(solution)/shard_map/all_to_all | solution.py:17
  127.8 2.6 reduce_sum.19
  130.4 0.2 multiply_convert_fusion
  130.6 0.4 concatenate.14
  131.0 0.2 broadcast_in_dim.2
  131.1 26.0 %all_to_all.22 = bf16[4,24,4,2,1344]{4,1,2,3,0:T(8,128)(2,1)S(1)} all-to-all(bf16[4,24,4,2,1344]{4,1,2,3,0:T(8,128)(2,1)S(1)} %broadcast_in_dim.2), channel_id=1, replica_groups=mesh['dp'=4,'expert'=4,'tensor'=16] {'dp'}, dimensions={0} | all-to-all | bytes 4128768 | tf_op jit(solution)/shard_map/all_to_all | solution.py:29
  157.2 0.2 copy.18
  157.4 0.0 copy-start.5
  157.4 1.0 fusion.9
  158.4 1.2 copy-done.5
  159.6 1.0 convolution_bitcast_fusion
  160.6 0.5 copy-done.7
  161.1 1.1 add_bitcast_fusion
  162.2 3.1 pad_maximum_fusion
  165.3 83.2 %all-reduce.1 = bf16[96,4,2,2048]{3,0,1,2:T(8,128)(2,1)} all-reduce(f32[96,4,2,2048]{3,0,1,2:T(8,128)} %pad_maximum_fusion), channel_id=1, replica_groups=mesh['dp'=4,'expert'=4,'tensor'=16] {'tensor'}, use_global_device_ids=true, to_apply=%region_4.5 | all-reduce | flops 1572864 | bytes 9437184 | tf_op jit(solution)/shard_map/psum | solution.py:93
  248.4 4.0 %copy.19 = bf16[96,4,2,2048]{3,0,2,1:T(8,128)(2,1)} copy(bf16[96,4,2,2048]{3,0,1,2:T(8,128)(2,1)} %all-reduce.1) | data formatting | bytes 6291456 | tf_op jit(solution)/shard_map/convert_element_type | solution.py:93
  252.4 4.8 %all-to-all-start.3 = ((bf16[96,4,2,2048]{3,0,2,1:T(8,128)(2,1)}), bf16[96,4,2,2048]{3,0,2,1:T(8,128)(2,1)}, u32[]{:S(2)}, u32[]{:S(2)}) async-start(bf16[96,4,2,2048]{3,0,2,1:T(8,128)(2,1)} %copy.19), calls=%async_computation.3 | async-start | bytes 6291456 | tf_op jit(solution)/shard_map/all_to_all | solution.py:94
  257.3 0.0 copy-start.9
  257.3 3.7 %bitcast_convert_fusion = bf16[2,448,1024]{2,1,0:T(8,128)(2,1)} fusion(bf16[96,4,2,1024]{3,0,2,1:T(8,128)(2,1)S(1)} %copy-done.11, bf16[96,4,2,1344]{3,0,1,2:T(8,128)(2,1)} %bitcast.65), kind=kOutput, calls=%fused_computation.1 | convolution fusion | flops 705560576 | bytes 4194304 | tf_op jit(solution)/shard_map/msjf,msjd->jfd/dot_general | solution.py:87
  261.0 2.4 bitcast_convert_fusion.1
  263.4 2.5 bitcast_convert_fusion.2
  265.9 26.3 %all-to-all-done.3 = bf16[96,4,2,2048]{3,0,2,1:T(8,128)(2,1)} async-done(((bf16[96,4,2,2048]{3,0,2,1:T(8,128)(2,1)}), bf16[96,4,2,2048]{3,0,2,1:T(8,128)(2,1)}, u32[]{:S(2)}, u32[]{:S(2)}) %all-to-all-start.3) | async-done | bytes 3145760 | tf_op jit(solution)/shard_map/all_to_all | solution.py:94
  292.2 6.8 %copy.20 = bf16[96,4,2,2048]{3,2,1,0:T(2,128)(2,1)} copy(bf16[96,4,2,2048]{3,0,2,1:T(8,128)(2,1)} %all-to-all-done.3) | data formatting | bytes 6291456 | tf_op jit(solution)/shard_map/all_to_all | solution.py:94
  299.0 5.7 %reshape.60 = bf16[768,2048]{1,0:T(8,128)(2,1)} reshape(bf16[96,4,2,2048]{3,2,1,0:T(2,128)(2,1)} %copy.20) | data formatting | bytes 6291456 | tf_op jit(solution)/shard_map/reshape | solution.py:95
  304.7 3.9 %convolution_convert_fusion.1 = bf16[512,2048]{1,0:T(8,128)(2,1)S(1)} fusion(bf16[768,2048]{1,0:T(8,128)(2,1)} %reshape.60, s32[512]{0:T(512)S(1)} %bitcast.72), kind=kOutput, calls=%fused_computation.6 | convolution fusion | flops 1612054528 | bytes 5244928 | tf_op jit(solution)/shard_map/dot_general | solution.py:96
  308.6 1.5 fusion.43
  (18 shorter events, 0.1 us)
Async XLA Ops:
  0.6 60.3 %copy-start = (bf16[2,1024,448]{1,2,0:T(8,128)(2,1)S(1)}, bf16[2,1024,448]{1,2,0:T(8,128)(2,1)}, u32[]{:S(2)}) copy-start(bf16[2,1024,448]{1,2,0:T(8,128)(2,1)} %param.9) | copy-start | bytes 5505028
  60.9 1.1 copy-start.8
  60.9 4.8 %copy-start.10 = (bf16[96,4,2,1024]{3,0,2,1:T(8,128)(2,1)}, bf16[96,4,2,1024]{3,0,2,1:T(8,128)(2,1)S(1)}, u32[]{:S(2)}) copy-start(bf16[96,4,2,1024]{3,0,2,1:T(8,128)(2,1)S(1)} %get-tuple-element.5) | copy-start | bytes 4718596
  60.9 2.6 copy-start.6
  63.5 2.1 copy-start.4
  157.4 3.3 %copy-start.2 = (bf16[4,24,4,2,1344]{4,1,0,2,3:T(8,128)(2,1)}, bf16[4,24,4,2,1344]{4,1,0,2,3:T(8,128)(2,1)S(1)}, u32[]{:S(2)}) copy-start(bf16[4,24,4,2,1344]{4,1,0,2,3:T(8,128)(2,1)S(1)} %copy.18) | copy-start | bytes 6193156
  157.4 2.3 copy-start.5
  159.6 1.5 copy-start.7
  252.4 4.8 %copy-start.12 = (s32[512,1]{0,1:T(1,128)S(1)}, s32[512,1]{0,1:T(1,128)}, u32[]{:S(2)}) copy-start(s32[512,1]{0,1:T(1,128)} %param.7) | copy-start | bytes 6148
  252.4 4.8 %copy-start.11 = (bf16[96,4,2,1024]{3,0,2,1:T(8,128)(2,1)S(1)}, bf16[96,4,2,1024]{3,0,2,1:T(8,128)(2,1)}, u32[]{:S(2)}) copy-start(bf16[96,4,2,1024]{3,0,2,1:T(8,128)(2,1)} %copy-done.10) | copy-start | bytes 4718596
  252.4 39.7 %all-to-all-start.3 = ((bf16[96,4,2,2048]{3,0,2,1:T(8,128)(2,1)}), bf16[96,4,2,2048]{3,0,2,1:T(8,128)(2,1)}, u32[]{:S(2)}, u32[]{:S(2)}) async-start(bf16[96,4,2,2048]{3,0,2,1:T(8,128)(2,1)} %copy.19), calls=%async_computation.3 | async-start | bytes 6291456 | tf_op jit(solution)/shard_map/all_to_all | solution.py:94
  257.2 3.7 %copy-start.3 = (bf16[4,24,4,2,1344]{4,1,0,2,3:T(8,128)(2,1)S(1)}, bf16[4,24,4,2,1344]{4,1,0,2,3:T(8,128)(2,1)}, u32[]{:S(2)}) copy-start(bf16[4,24,4,2,1344]{4,1,0,2,3:T(8,128)(2,1)} %copy-done.2) | copy-start | bytes 6193156
  257.3 3.7 %copy-start.9 = (bf16[96,4,2,1024]{3,0,2,1:T(8,128)(2,1)S(1)}, bf16[96,4,2,1024]{3,0,2,1:T(8,128)(2,1)}, u32[]{:S(2)}) copy-start(bf16[96,4,2,1024]{3,0,2,1:T(8,128)(2,1)} %copy-done.8) | copy-start | bytes 4718596
  304.7 5.4 %copy-start.1 = (bf16[2,1024,448]{1,2,0:T(8,128)(2,1)S(1)}, bf16[2,1024,448]{1,2,0:T(8,128)(2,1)}, u32[]{:S(2)}) copy-start(bf16[2,1024,448]{1,2,0:T(8,128)(2,1)} %param.9) | copy-start | bytes 5505028
where the time goes:
time: 313 us; the launch traced here: 310 us
  blocking collectives  203 us (65%)
  local copies, waits for them, and re-layouts  40.4 us (13%)
  waiting for transfers between devices  26.3 us (8%)
  matrix products  25.8 us (8%)
  other arithmetic  9.35 us (3%)
  starting transfers between devices  4.77 us (2%)
    psum x1, blocking collectives, body(): summed = lax.psum(rows_out, 'tensor').astype(jnp.bfloat16)  83.2 us
    all_to_all x1, blocking collectives, summed_on_arrival(): tiles = lax.all_to_all(split_up(shard, dim, count), axis, 0, 0, tiled=True)  51.8 us
    all_to_all x1, blocking collectives, body(): lax.all_to_all(packed, 'expert', split_axis=1, concat_axis=1, tiled=True)  41.5 us
    all_to_all x1, waiting for transfers between devices, body(): lax.all_to_all(summed, 'expert', split_axis=1, concat_axis=1, tiled=True)  26.3 us
    all_to_all x1, blocking collectives, sent_to_all(): lax.all_to_all(jnp.broadcast_to(shard[None], (count, *shard.shape)), axis...  26 us
    reshape x2, local copies, waits for them, and re-layouts, body(): packed = packed.reshape(MOST, groups, local_experts, 2 * feat_width)  9.61 us
    all_to_all x1, local copies, waits for them, and re-layouts, body(): lax.all_to_all(summed, 'expert', split_axis=1, concat_axis=1, tiled=True)  6.84 us
  transfers between devices with their start and end apart: 1, of which 1 were waited for; matrix products, arithmetic and copies ran while one was open for 3% of the time, Pallas kernels for 0%

commit v1 on v0

v1 whole, which is shorter than its diff:
```python
import jax
import jax.numpy as jnp
from jax import lax
from jax.experimental import pallas as pl
from jax.experimental.pallas import tpu as pltpu
from jax.sharding import PartitionSpec as P

MOST = 96
NX, NY, NZ = 4, 4, 8
TOK = 512
FEAT = 1024
HID = 448
SLICE = HID // NX
ROWS = NY * MOST
COL = FEAT // NZ
BF = jnp.bfloat16
F32 = jnp.float32
MESH = pl.DeviceIdType.MESH


def nt(a, b):
    return lax.dot_general(a, b, (((1,), (1,)), ((), ())), preferred_element_type=F32)


def tn(a, b):
    return lax.dot_general(a, b, (((0,), (0,)), ((), ())), preferred_element_type=F32)


def nn(a, b):
    return jnp.dot(a, b, preferred_element_type=F32)


class RingGather:
    def __init__(self, region, z, right, left, sibling, sems, plus, minus):
        self.region, self.z = region, z
        self.dev = (right, left)
        self.sibling = sibling
        self.zs, self.zr, self.ss, self.sr = sems
        self.count = (plus, minus)
        self.sent = []
        self.hops = ({}, {})
        self.twins = []

    def chunk(self, way, hop):
        return lax.rem(self.z + (NZ - hop if way == 0 else hop), NZ)

    def send(self, way, hop):
        part = self.region(self.chunk(way, hop))
        copy = pltpu.make_async_remote_copy(
            part, part, self.zs.at[way, hop], self.zr.at[way, hop], self.dev[way], MESH
        )
        copy.start()
        self.hops[way][hop] = copy

    def twin(self, chunk, number):
        part = self.region(chunk)
        copy = pltpu.make_async_remote_copy(
            part, part, self.ss.at[number], self.sr.at[number], self.sibling, MESH
        )
        copy.start()
        self.twins.append(copy)

    def start(self):
        for way in (0, 1):
            self.send(way, 0)
        self.twin(self.z, 0)

    def step(self, hop):
        for way in (0, 1):
            if hop < self.count[way]:
                self.hops[way][hop].wait_recv()
                if hop + 1 < self.count[way]:
                    self.send(way, hop + 1)
                self.twin(self.chunk(way, hop + 1), 1 + hop + (self.count[0] if way else 0))

    def finish(self):
        for copy in self.twins:
            copy.wait_recv()

    def drain(self):
        for way in (0, 1):
            for copy in self.hops[way].values():
                copy.wait_send()
        for copy in self.twins:
            copy.wait_send()


def kernel(
    lab_ref,
    tok_hbm,
    go_hbm,
    wg_hbm,
    wu_hbm,
    wd_hbm,
    mix_hbm,
    gt_hbm,
    gg_hbm,
    gu_hbm,
    gd_hbm,
    src,
    w,
    slots,
    outgo,
    x,
    part,
    part16,
    via,
    joined,
    got,
    acts,
    keep,
    twin_out,
    twin_in,
    rows_out,
    ring_out,
    ring_in,
    final,
    home,
    out,
    wgrad,
    load_sem,
    store_sem,
    y_s,
    y_r,
    az_s,
    az_r,
    as_s,
    as_r,
    b_s,
    b_r,
    c_s,
    c_r,
    t_s,
    t_r,
    r_s,
    r_r,
    h_s,
    h_r,
    gz_s,
    gz_r,
    gs_s,
    gs_r,
):
    d = lax.axis_index("dp")
    g = lax.axis_index("expert")
    t = lax.axis_index("tensor")
    z = lax.div(t, 2)
    c = lax.rem(t, 2)
    other = 1 - c
    right = lax.rem(d + 1, NX)
    left = lax.rem(d + NX - 1, NX)
    far = lax.rem(d + 2, NX)
    z_up = {"tensor": lax.rem(z + 1, NZ) * 2 + c}
    z_down = {"tensor": lax.rem(z + NZ - 1, NZ) * 2 + c}
    sibling = {"tensor": z * 2 + other}
    x_dev = ({"dp": right}, {"dp": left})
    group = [lax.rem(g + o, NY) for o in range(NY)]

    def cols(q):
        return pl.ds(pl.multiple_of(q * COL, COL), COL)

    def rows(q):
        return pl.ds(pl.multiple_of(q * SLICE, 16), SLICE)

    barrier = pltpu.get_barrier_semaphore()
    greet = [z_up, z_down, sibling, x_dev[0], x_dev[1]]
    for o in range(1, NY):
        greet.append({"expert": group[o]})
        greet.append({"expert": group[o], "tensor": z * 2 + other})
    for peer in greet:
        pl.semaphore_signal(barrier, inc=1, device_id=peer, device_id_type=MESH)

    loads = [
        pltpu.make_async_copy(tok_hbm, src.at[0], load_sem.at[0]),
        pltpu.make_async_copy(go_hbm, src.at[1], load_sem.at[1]),
        pltpu.make_async_copy(wg_hbm, w.at[0], load_sem.at[2]),
        pltpu.make_async_copy(wu_hbm, w.at[1], load_sem.at[3]),
        pltpu.make_async_copy(wd_hbm, w.at[2], load_sem.at[4]),
    ]
    for copy in loads:
        copy.start()

    lab = lab_ref[...]
    onehot = jnp.where(
        lax.broadcasted_iota(jnp.int32, (8, TOK), 0) == lab, 1.0, 0.0
    )
    earlier = jnp.where(
        lax.broadcasted_iota(jnp.int32, (TOK, TOK), 0)
        < lax.broadcasted_iota(jnp.int32, (TOK, TOK), 1),
        1.0,
        0.0,
    ).astype(BF)
    rank = jnp.sum(nn(onehot.astype(BF), earlier) * onehot, axis=0, keepdims=True)
    relative = ((lab >> 1) - g + NY) & (NY - 1)
    place = relative.astype(F32) * float(MOST) + rank
    spot = lax.broadcasted_iota(jnp.int32, (ROWS, TOK), 0).astype(F32)
    for j in range(2):
        mine = jnp.where((lab & 1) == j, place, -1.0)
        slots[j] = jnp.where(spot == mine, 1.0, 0.0).astype(BF)

    y_copies = [[], []]

    def dispatch(k):
        loads[k].wait()
        picked = nn(slots[c, pl.ds(MOST, ROWS - MOST)], src[k, :, cols(z)])
        outgo[k] = picked.astype(BF)
        if k == 0:
            pl.semaphore_wait(barrier, len(greet))
        for o in (1, 3, 2):
            back = NY - o
            copy = pltpu.make_async_remote_copy(
                outgo.at[k, pl.ds((o - 1) * MOST, MOST)],
                x.at[k, c, pl.ds(back * MOST, MOST), cols(z)],
                y_s.at[k, o - 1],
                y_r.at[k, o - 1],
                {"expert": group[o]},
                MESH,
            )
            copy.start()
            y_copies[k].append(copy)

    def own_rows(k):
        for j in range(2):
            x[k, j, pl.ds(0, MOST)] = nn(slots[j, pl.ds(0, MOST)], src[k]).astype(BF)

    gathers = [
        RingGather(
            lambda q, k=k: x.at[k, c, pl.ds(MOST, ROWS - MOST), cols(q)],
            z,
            z_up,
            z_down,
            sibling,
            (az_s.at[k], az_r.at[k], as_s.at[k], as_r.at[k]),
            *((4, 3) if k == 0 else (3, 4)),
        )
        for k in range(2)
    ]

    def begin(k):
        for copy in y_copies[k]:
            copy.wait_recv()
        gathers[k].start()

    b_copies = {}

    def push(table, key, source, target, send, recv, way):
        copy = pltpu.make_async_remote_copy(source, target, send, recv, x_dev[way], MESH)
        copy.start()
        table[key] = copy

    def partial(k):
        inputs = 1 if k == 2 else 0

        @pl.loop(0, 2)
        def _(j):
            value = nt(w[k, j], x[inputs, j])
            part[k, j] = value
            part16[k, j] = value.astype(BF)

        for way, (near, j) in enumerate(((right, 0), (left, 1))):
            push(
                b_copies, (k, way, 0), part16.at[k, j, rows(far)], via.at[k, way],
                b_s.at[k, way, 0], b_r.at[k, way, 0], way,
            )
        for way, (near, j) in enumerate(((right, 0), (left, 1))):
            push(
                b_copies, (k, way, 1), part16.at[k, 1 - j, rows(near)], got.at[k, way, 1 - j],
                b_s.at[k, way, 1], b_r.at[k, way, 1], way,
            )

    def join(k):
        for way, (near, j) in enumerate(((right, 0), (left, 1))):
            b_copies[k, way, 0].wait_recv()
            joined[k, way] = (part[k, j, rows(near)] + via[k, way].astype(F32)).astype(BF)
            push(
                b_copies, (k, way, 2), joined.at[k, way], got.at[k, way, j],
                b_s.at[k, way, 2], b_r.at[k, way, 2], way,
            )

    def arrived(k):
        for way in (0, 1):
            for piece in (1, 2):
                b_copies[k, way, piece].wait_recv()

    def total(k, j):
        return part[k, j, rows(d)] + got[k, 0, j].astype(F32) + got[k, 1, j].astype(F32)

    c_copies = {}

    def share(n):
        for piece in (0, 1):
            for way in (0, 1):
                j = piece ^ way
                block = acts.at[n, j, rows(d)]
                push(
                    c_copies, (n, way, piece), block, block,
                    c_s.at[n, way, piece], c_r.at[n, way, piece], way,
                )

    def relay(n):
        for way, origin in enumerate((left, right)):
            c_copies[n, way, 0].wait_recv()
            block = acts.at[n, way, rows(origin)]
            push(
                c_copies, (n, way, 2), block, block,
                c_s.at[n, way, 2], c_r.at[n, way, 2], way,
            )

    def shared(n):
        for way in (0, 1):
            for piece in (1, 2):
                c_copies[n, way, piece].wait_recv()

    def forward_acts():
        for j in range(2):
            gate = total(0, j)
            up = total(1, j)
            sig = jax.nn.sigmoid(gate)
            active = gate * sig
            acts[0, j, rows(d)] = (active * up).astype(BF)
            keep[0, j] = up * (sig * (1.0 + gate * (1.0 - sig)))
            keep[1, j] = active
        share(0)

    def backward_acts():
        for j in range(2):
            back = total(2, j)
            acts[1, j, rows(d)] = (back * keep[0, j]).astype(BF)
            acts[2, j, rows(d)] = (back * keep[1, j]).astype(BF)
        share(1)
        share(2)

    def rows_of(kd, j):
        if kd == 0:
            return tn(acts[0, j], w[2, j])
        return tn(acts[1, j], w[0, j]) + tn(acts[2, j], w[1, j])

    t_copies = []

    def expand(kd):
        twin_out[kd] = rows_of(kd, other)
        copy = pltpu.make_async_remote_copy(
            twin_out.at[kd], twin_in.at[kd], t_s.at[kd], t_r.at[kd], sibling, MESH
        )
        copy.start()
        t_copies.append(copy)
        rows_out[kd] = rows_of(kd, c)

    ring = {}
    counts = ((4, 3), (3, 4))

    def chunk_sum(kd, q):
        return rows_out[kd, :, cols(q)] + twin_in[kd, :, cols(q)]

    def reduce_step(kd, i):
        if i == 0:
            t_copies[kd].wait_recv()
        for way in (0, 1):
            n = counts[kd][way]
            if i >= n:
                continue
            ahead = n - i
            q = lax.rem(z + (ahead if way == 0 else NZ - ahead), NZ)
            value = chunk_sum(kd, q)
            if i > 0:
                ring[kd, way, i - 1].wait_recv()
                value = value + ring_in[kd, way, i - 1].astype(F32)
            ring_out[kd, way, i] = value.astype(BF)
            copy = pltpu.make_async_remote_copy(
                ring_out.at[kd, way, i], ring_in.at[kd, way, i],
                r_s.at[kd, way, i], r_r.at[kd, way, i],
                (z_up, z_down)[way], MESH,
            )
            copy.start()
            ring[kd, way, i] = copy

    h_copies = [[], []]

    def go_home(kd):
        value = chunk_sum(kd, z)
        for way in (0, 1):
            last = counts[kd][way] - 1
            ring[kd, way, last].wait_recv()
            value = value + ring_in[kd, way, last].astype(F32)
        value = value.astype(BF)
        final[kd] = value
        home[kd, c, pl.ds(0, MOST)] = value[:MOST]
        for o in (2, 1, 3, 0):
            back = (NY - o) % NY
            for same in (0, 1):
                if o == 0 and same == 0:
                    continue
                core = c if same == 0 else other
                copy = pltpu.make_async_remote_copy(
                    final.at[kd, pl.ds(o * MOST, MOST)],
                    home.at[kd, c, pl.ds(back * MOST, MOST)],
                    h_s.at[kd, same, o],
                    h_r.at[kd, same, o],
                    {"expert": group[o], "tensor": z * 2 + core},
                    MESH,
                )
                copy.start()
                h_copies[kd].append(copy)

    half = pl.ds(pl.multiple_of(c * (TOK // 2), TOK // 2), TOK // 2)
    outs = [
        RingGather(
            lambda q, kd=kd: out.at[kd, half, cols(q)],
            z,
            z_up,
            z_down,
            sibling,
            (gz_s.at[kd], gz_r.at[kd], gs_s.at[kd], gs_r.at[kd]),
            *counts[kd],
        )
        for kd in range(2)
    ]

    def settle(kd):
        for copy in h_copies[kd]:
            copy.wait_recv()
        value = tn(slots[0, :, half], home[kd, 0]) + tn(slots[1, :, half], home[kd, 1])
        out[kd, half, cols(z)] = value.astype(BF)
        outs[kd].start()

    stores = []

    def store(source, target, number):
        copy = pltpu.make_async_copy(source, target, store_sem.at[number])
        copy.start()
        stores.append(copy)

    def weight_grad(n, k, target):
        @pl.loop(0, 2)
        def _(j):
            wgrad[n, j] = nn(acts[n, j], x[k, j]).astype(BF)

        store(wgrad.at[n], target, n)

    dispatch(0)
    dispatch(1)
    own_rows(0)
    begin(0)
    own_rows(1)
    gathers[0].step(0)
    begin(1)
    gathers[0].step(1)
    gathers[1].step(0)
    gathers[0].step(2)
    gathers[1].step(1)
    gathers[0].step(3)
    gathers[0].finish()
    loads[2].wait()
    partial(0)
    gathers[1].step(2)
    loads[3].wait()
    partial(1)
    join(0)
    gathers[1].step(3)
    gathers[1].finish()
    join(1)
    loads[4].wait()
    partial(2)
    arrived(0)
    arrived(1)
    forward_acts()
    join(2)
    relay(0)
    arrived(2)
    backward_acts()
    shared(0)
    expand(0)
    reduce_step(0, 0)
    relay(1)
    relay(2)
    reduce_step(0, 1)
    weight_grad(0, 1, gd_hbm)
    reduce_step(0, 2)
    shared(1)
    shared(2)
    reduce_step(0, 3)
    expand(1)
    go_home(0)
    reduce_step(1, 0)
    reduce_step(1, 1)
    settle(0)
    weight_grad(1, 0, gg_hbm)
    reduce_step(1, 2)
    outs[0].step(0)
    reduce_step(1, 3)
    outs[0].step(1)
    go_home(1)
    weight_grad(2, 0, gu_hbm)
    outs[0].step(2)
    settle(1)
    outs[0].step(3)
    outs[1].step(0)
    outs[0].finish()
    store(out.at[0], mix_hbm, 3)
    for hop in (1, 2, 3):
        outs[1].step(hop)
    outs[1].finish()
    store(out.at[1], gt_hbm, 4)

    for ring_gather in gathers + outs:
        ring_gather.drain()
    for copy in y_copies[0] + y_copies[1] + t_copies + h_copies[0] + h_copies[1]:
        copy.wait_send()
    for table in (b_copies, c_copies, ring):
        for copy in table.values():
            copy.wait_send()
    for copy in stores:
        copy.wait()


def body(tokens, labels, grad_out, w_gate, w_up, w_down):
    dma = pltpu.SemaphoreType.DMA
    scratch = [
        pltpu.VMEM((2, TOK, FEAT), BF),
        pltpu.VMEM((3, 2, HID, FEAT), BF),
        pltpu.VMEM((2, ROWS, TOK), BF),
        pltpu.VMEM((2, ROWS - MOST, COL), BF),
        pltpu.VMEM((2, 2, ROWS, FEAT), BF),
        pltpu.VMEM((3, 2, HID, ROWS), F32),
        pltpu.VMEM((3, 2, HID, ROWS), BF),
        pltpu.VMEM((3, 2, SLICE, ROWS), BF),
        pltpu.VMEM((3, 2, SLICE, ROWS), BF),
        pltpu.VMEM((3, 2, 2, SLICE, ROWS), BF),
        pltpu.VMEM((3, 2, HID, ROWS), BF),
        pltpu.VMEM((2, 2, SLICE, ROWS), F32),
        pltpu.VMEM((2, ROWS, FEAT), F32),
        pltpu.VMEM((2, ROWS, FEAT), F32),
        pltpu.VMEM((2, ROWS, FEAT), F32),
        pltpu.VMEM((2, 2, 4, ROWS, COL), BF),
        pltpu.VMEM((2, 2, 4, ROWS, COL), BF),
        pltpu.VMEM((2, ROWS, COL), BF),
        pltpu.VMEM((2, 2, ROWS, COL), BF),
        pltpu.VMEM((2, TOK, FEAT), BF),
        pltpu.VMEM((3, 2, HID, FEAT), BF),
        dma((5,)),
        dma((5,)),
        dma((2, 3)),
        dma((2, 3)),
        dma((2, 2, 4)),
        dma((2, 2, 4)),
        dma((2, 8)),
        dma((2, 8)),
        dma((3, 2, 3)),
        dma((3, 2, 3)),
        dma((3, 2, 3)),
        dma((3, 2, 3)),
        dma((2,)),
        dma((2,)),
        dma((2, 2, 4)),
        dma((2, 2, 4)),
        dma((2, 2, 4)),
        dma((2, 2, 4)),
        dma((2, 2, 4)),
        dma((2, 2, 4)),
        dma((2, 8)),
        dma((2, 8)),
    ]
    anywhere = pl.BlockSpec(memory_space=pl.ANY)
    mixed, grad_tokens, gate_t, up_t, down = pl.pallas_call(
        kernel,
        out_shape=(
            jax.ShapeDtypeStruct((TOK, FEAT), BF),
            jax.ShapeDtypeStruct((TOK, FEAT), BF),
            jax.ShapeDtypeStruct((2, HID, FEAT), BF),
            jax.ShapeDtypeStruct((2, HID, FEAT), BF),
            jax.ShapeDtypeStruct((2, HID, FEAT), BF),
        ),
        in_specs=[pl.BlockSpec(memory_space=pltpu.VMEM)] + [anywhere] * 5,
        out_specs=(anywhere,) * 5,
        scratch_shapes=scratch,
        compiler_params=pltpu.CompilerParams(
            collective_id=0, has_side_effects=True, vmem_limit_bytes=50 * 1024 * 1024
        ),
    )(
        labels.reshape(1, TOK),
        tokens,
        grad_out,
        jnp.swapaxes(w_gate, 1, 2),
        jnp.swapaxes(w_up, 1, 2),
        w_down,
    )
    return mixed, grad_tokens, jnp.swapaxes(gate_t, 1, 2), jnp.swapaxes(up_t, 1, 2), down


def solution(mesh):
    in_specs = (
        P("expert", "dp"),
        P("expert", None),
        P("expert", "dp"),
        P("expert", "dp", "tensor"),
        P("expert", "dp", "tensor"),
        P("expert", "tensor", "dp"),
    )
    out_specs = (
        P("expert", "dp"),
        P("expert", "dp"),
        P("expert", "dp", "tensor"),
        P("expert", "dp", "tensor"),
        P("expert", "tensor", "dp"),
    )
    return jax.shard_map(body, mesh=mesh, in_specs=in_specs, out_specs=out_specs, check_vma=False)
```

time: 313 us -> 125 us (0.40)
  blocking collectives: 203 us -> 0 us
  Pallas kernels: 0 us -> 115 us
  local copies, waits for them, and re-layouts: 40.4 us -> 9.39 us
  waiting for transfers between devices: 26.3 us -> 0 us
  matrix products: 25.8 us -> 0 us
  other arithmetic: 9.35 us -> 0 us
  starting transfers between devices: 4.77 us -> 0 us
    all_to_all x3 -> x0, blocking collectives: 119 us -> none  [the longest x1 51.8 us: summed_on_arrival(): tiles = lax.all_to_all(split_up(shard, dim, count), axis, 0, 0, tiled=True)]
    pallas_call x0 -> x1, Pallas kernels: none -> 115 us  [body(): pl.pallas_call(kernel, out_shape=(jax.ShapeDtypeStruct((TOK, FEAT), BF),...]
    psum x1 -> x0, blocking collectives: 83.2 us -> none  [body(): summed = lax.psum(rows_out, 'tensor').astype(jnp.bfloat16)]
    all_to_all x1 -> x0, waiting for transfers between devices: 26.3 us -> none  [body(): lax.all_to_all(summed, 'expert', split_axis=1, concat_axis=1, tiled=True)]
    dot_general x11 -> x0, matrix products: 25.8 us -> none  [the longest x1 4.99 us: body(): jnp.dot(to_slots, payload, preferred_element_type=jnp.float32)]
    reshape x4 -> x0, local copies, waits for them, and re-layouts: 17.9 us -> none  [the longest x2 9.61 us: body(): packed = packed.reshape(MOST, groups, local_experts, 2 * feat_width)]
    all_to_all x2 -> x0, local copies, waits for them, and re-layouts: 7.01 us -> none  [the longest x1 6.84 us: body(): lax.all_to_all(summed, 'expert', split_axis=1, concat_axis=1, tiled=True)]
    unnamed x26 -> x15, local copies, waits for them, and re-layouts: 3.35 us -> 9.39 us
  transfers between devices with their start and end apart: 1 -> 0, of which waited for: 1 -> 0; matrix products, arithmetic and copies ran while one was open for 3% -> 0% of each run, Pallas kernels for 0% -> 0%
where the time goes in v1:
time: 125 us
  Pallas kernels  115 us (92%)
  local copies, waits for them, and re-layouts  9.39 us (8%)
    pallas_call x1, Pallas kernels, body(): pl.pallas_call(kernel, out_shape=(jax.ShapeDtypeStruct((TOK, FEAT), BF),...  115 us
    unnamed x15, local copies, waits for them, and re-layouts  9.39 us

profile of v1, /device:TPU:1, one launch (start us, length us, event | category | flops | bytes accessed | tf_op | source)
XLA Modules:
  0.0 125.1 jit_solution(2645121445030125012)
XLA Ops:
  0.6 0.0 copy-start
  0.6 1.2 copy-done
  1.9 0.0 copy-start.1
  1.9 0.7 copy-done.1
  2.5 115.0 %shard_map.101 = (bf16[512,1024]{1,0:T(8,128)(2,1)S(1)}, bf16[512,1024]{1,0:T(8,128)(2,1)S(1)}, bf16[2,448,1024]{2,1,0:T(8,128)(2,1)}, bf16[2,448,1024]{2,1,0:T(8,128)(2,1)}, bf16[2,448,1024]{2,1,0:T(8,128)(2,1)}) custom-call(s32[1,512]{1,0:T(1,128)S(1)} %bitcast.5, bf16[512,1024]{1,0:T(8,128)(2,1)S(1)} %copy-done, bf16[512,1024]{1,0:T(8,128)(2,1)} %go_hbm.1, ...), custom_call_target="tpu_custom_call" | custom-call | tf_op jit(solution)/shard_map/pallas_call | solution.py:564
  117.5 0.0 copy-start.4
  117.6 1.0 copy.16
  118.5 1.0 copy.17
  119.5 0.0 copy-done.4
  119.5 0.0 copy-start.3
  119.5 1.2 copy.18
  120.7 0.9 copy-done.3
  121.7 0.0 copy-start.2
  121.7 1.2 copy.19
  122.9 0.9 copy-done.2
  123.8 1.2 copy.20
Async XLA Ops:
  0.6 1.2 copy-start
  1.9 0.7 copy-start.1
  117.5 2.0 %copy-start.4 = (bf16[2,448,1024]{2,1,0:T(8,128)(2,1)S(1)}, bf16[2,448,1024]{2,1,0:T(8,128)(2,1)}, u32[]{:S(2)}) copy-start(bf16[2,448,1024]{2,1,0:T(8,128)(2,1)} %get-tuple-element.12) | copy-start | bytes 5505028
  119.5 2.2 %copy-start.3 = (bf16[2,448,1024]{2,1,0:T(8,128)(2,1)S(1)}, bf16[2,448,1024]{2,1,0:T(8,128)(2,1)}, u32[]{:S(2)}) copy-start(bf16[2,448,1024]{2,1,0:T(8,128)(2,1)} %get-tuple-element.13) | copy-start | bytes 5505028
  121.7 2.2 %copy-start.2 = (bf16[2,448,1024]{2,1,0:T(8,128)(2,1)S(1)}, bf16[2,448,1024]{2,1,0:T(8,128)(2,1)}, u32[]{:S(2)}) copy-start(bf16[2,448,1024]{2,1,0:T(8,128)(2,1)} %get-tuple-element.24) | copy-start | bytes 5505028

commit v2 on v0

v2 whole, which is shorter than its diff:
```python
import jax
import jax.numpy as jnp
from jax import lax
from jax.experimental import pallas as pl
from jax.experimental.pallas import tpu as pltpu
from jax.sharding import PartitionSpec as P

MOST = 96
NX, NY, NZ = 4, 4, 8
TOK = 512
FEAT = 1024
HID = 448
SLICE = HID // NX
ROWS = NY * MOST
COL = FEAT // NZ
PART = FEAT // 2
SHARE = MOST // 2
HALF = NY * SHARE
BF = jnp.bfloat16
F32 = jnp.float32
MESH = pl.DeviceIdType.MESH


def nt(a, b):
    return lax.dot_general(a, b, (((1,), (1,)), ((), ())), preferred_element_type=F32)


def tn(a, b):
    return lax.dot_general(a, b, (((0,), (0,)), ((), ())), preferred_element_type=F32)


def nn(a, b):
    return jnp.dot(a, b, preferred_element_type=F32)


def take(ref, sem):
    pltpu.make_async_copy(ref, ref, sem).wait()


class RingGather:
    def __init__(self, region, z, right, left, sibling, sems, plus, minus):
        self.region, self.z = region, z
        self.dev = (right, left)
        self.sibling = sibling
        self.zs, self.zr, self.ss, self.sr = sems
        self.count = (plus, minus)

    def chunk(self, way, hop):
        return lax.rem(self.z + (NZ - hop if way == 0 else hop), NZ)

    def number(self, way, hop):
        return hop + (self.count[0] if way else 0)

    def send(self, way, hop):
        part = self.region(self.chunk(way, hop))
        pltpu.make_async_remote_copy(
            part, part, self.zs, self.zr.at[self.number(way, hop)], self.dev[way], MESH
        ).start()

    def twin(self, chunk):
        part = self.region(chunk)
        pltpu.make_async_remote_copy(part, part, self.ss, self.sr, self.sibling, MESH).start()

    def start(self):
        for way in (0, 1):
            self.send(way, 0)
        self.twin(self.z)

    def step(self, hop):
        for way in (0, 1):
            if hop < self.count[way]:
                chunk = self.chunk(way, hop + 1)
                take(self.region(chunk), self.zr.at[self.number(way, hop)])
                if hop + 1 < self.count[way]:
                    self.send(way, hop + 1)
                self.twin(chunk)


def kernel(
    lab_hbm,
    tok_hbm,
    go_hbm,
    wg_hbm,
    wu_hbm,
    wd_hbm,
    out,
    wgrad,
    lab_ref,
    src,
    w,
    slots,
    outgo,
    passing,
    x,
    part,
    part16,
    land,
    joined,
    acts,
    keep,
    twin_in,
    early_in,
    early_out,
    rows_out,
    ring_out,
    ring_in,
    final,
    home,
    load_sem,
    sent,
    y_r,
    z_r,
    w_r,
    v_r,
    b_r,
    c_r,
    f_r,
    t_r,
    e_r,
    r_r,
    h_r,
    gz_r,
    gs_r,
):
    d = lax.axis_index("dp")
    g = lax.axis_index("expert")
    t = lax.axis_index("tensor")
    z = lax.div(t, 2)
    c = lax.rem(t, 2)
    other = 1 - c
    right = lax.rem(d + 1, NX)
    left = lax.rem(d + NX - 1, NX)
    far = lax.rem(d + 2, NX)
    z_up = {"tensor": lax.rem(z + 1, NZ) * 2 + c}
    z_down = {"tensor": lax.rem(z + NZ - 1, NZ) * 2 + c}
    sibling = {"tensor": z * 2 + other}
    x_dev = ({"dp": right}, {"dp": left})
    s_y, s_z, s_w, s_b, s_c, s_t, s_e, s_r, s_h, s_gz, s_gs = [sent.at[i] for i in range(11)]
    group = [lax.rem(g + o, NY) for o in range(NY)]

    def cols(q):
        return pl.ds(pl.multiple_of(q * COL, COL), COL)

    def rows(q):
        return pl.ds(pl.multiple_of(q * SLICE, 16), SLICE)

    barrier = pltpu.get_barrier_semaphore()
    greet = [z_up, z_down, sibling, x_dev[0], x_dev[1]]
    for o in range(1, NY):
        greet.append({"expert": group[o]})
        greet.append({"expert": group[o], "tensor": z * 2 + other})
    for peer in greet:
        pl.semaphore_signal(barrier, inc=1, device_id=peer, device_id_type=MESH)

    loads = [
        pltpu.make_async_copy(tok_hbm, src.at[0], load_sem.at[0]),
        pltpu.make_async_copy(go_hbm, src.at[1], load_sem.at[1]),
        pltpu.make_async_copy(wg_hbm, w.at[0], load_sem.at[2]),
        pltpu.make_async_copy(wu_hbm, w.at[1], load_sem.at[3]),
        pltpu.make_async_copy(wd_hbm, w.at[2], load_sem.at[4]),
    ]
    labels = pltpu.make_async_copy(lab_hbm, lab_ref, load_sem.at[5])
    labels.start()
    for copy in loads:
        copy.start()

    earlier = jnp.where(
        lax.broadcasted_iota(jnp.int32, (TOK, TOK), 0)
        < lax.broadcasted_iota(jnp.int32, (TOK, TOK), 1),
        1.0,
        0.0,
    ).astype(BF)
    labels.wait()
    lab = lab_ref[...]
    onehot = jnp.where(
        lax.broadcasted_iota(jnp.int32, (8, TOK), 0) == lab, 1.0, 0.0
    )
    rank = jnp.sum(nn(onehot.astype(BF), earlier) * onehot, axis=0, keepdims=True)
    relative = ((lab >> 1) - g + NY) & (NY - 1)
    place = relative.astype(F32) * float(SHARE) + rank
    place = place + jnp.where(rank >= float(SHARE), float(HALF - SHARE), 0.0)
    spot = lax.broadcasted_iota(jnp.int32, (ROWS, TOK), 0).astype(F32)
    for j in range(2):
        mine = jnp.where((lab & 1) == j, place, -1.0)
        slots[j] = jnp.where(spot == mine, 1.0, 0.0).astype(BF)

    span = pl.ds(pl.multiple_of(lax.rem(z, 2) * PART, PART), PART)
    y_copies = {}

    def own(first, count):
        return pl.ds(pl.multiple_of(c * HALF + first * SHARE, 16), count * SHARE)

    def quarter(parity, way):
        start = parity * PART + way * (PART // 2)
        return pl.ds(pl.multiple_of(start, PART // 2), PART // 2)

    def pick(k):
        loads[k].wait()
        for j in range(2):
            outgo[k, j] = nn(slots[j, own(1, NY - 1)], src[k, :, span]).astype(BF)

    def remote(source, target, send, recv, device):
        pltpu.make_async_remote_copy(source, target, send, recv, device, MESH).start()

    onward = {"expert": lax.rem(g + 1 + 2 * c, NY)}
    other_span = pl.ds(pl.multiple_of(PART - lax.rem(z, 2) * PART, PART), PART)

    def launch_far(k):
        remote(outgo.at[k, :, pl.ds(SHARE, SHARE)], passing.at[k], s_y, y_r.at[k, 2], onward)

    def launch_near(k):
        for o in (1, 3):
            remote(
                outgo.at[k, :, pl.ds((o - 1) * SHARE, SHARE)],
                x.at[k, :, own(NY - o, 1), span],
                s_y, y_r.at[k, NY - o], {"expert": group[o]},
            )

    def pass_on(k):
        take(passing.at[k], y_r.at[k, 2])
        remote(passing.at[k], x.at[k, :, own(2, 1), span], s_y, y_r.at[k, 0], onward)

    def own_rows(k):
        for j in range(2):
            both = jnp.concatenate([slots[j, pl.ds(0, SHARE)], slots[j, pl.ds(HALF, SHARE)]], axis=0)
            value = nn(both, src[k]).astype(BF)
            x[k, j, pl.ds(0, SHARE)] = value[:SHARE]
            x[k, j, pl.ds(HALF, SHARE)] = value[SHARE:]

    def twin(k, block, columns):
        part_ref = x.at[k, :, own(block, 1), columns]
        remote(part_ref, part_ref, s_w, w_r.at[k], sibling)

    def spread(k, block):
        take(x.at[k, :, own(block, 1), span], y_r.at[k, 0 if block == 2 else block])
        for way in (0, 1):
            part_ref = x.at[k, :, own(block, 1), quarter(lax.rem(z, 2), way)]
            remote(part_ref, part_ref, s_z, z_r.at[k, block - 1], (z_up, z_down)[way])
        twin(k, block, span)

    def collect(k, block):
        take(x.at[k, :, own(block, 1), other_span], z_r.at[k, block - 1])
        twin(k, block, other_span)

    def complete(k):
        theirs_x = pl.ds(pl.multiple_of(other * HALF + SHARE, 16), HALF - SHARE)
        take(x.at[k, :, theirs_x], w_r.at[k])

    def partial(k):
        for j in range(2):
            value = nt(w[k, j], x[1 if k == 2 else 0, j])
            part[k, j] = value
            part16[k, j] = value.astype(BF)
            way = j
            remote(part16.at[k, j, rows(far)], land.at[k, way], s_b, v_r.at[k, way], x_dev[way])
            way = 1 - j
            remote(
                part16.at[k, j, rows((right, left)[way])], land.at[k, 2 + 2 * way + j],
                s_b, b_r.at[k], x_dev[way],
            )

    def join(k):
        for way in (0, 1):
            take(land.at[k, way], v_r.at[k, way])
            near = rows((right, left)[way])
            joined[k, way] = (part[k, way, near] + land[k, way].astype(F32)).astype(BF)
            remote(joined.at[k, way], land.at[k, 2 + 2 * way + way], s_b, b_r.at[k], x_dev[way])

    def arrived(k):
        take(land.at[k, pl.ds(2, 4)], b_r.at[k])

    def total(k, j):
        return part[k, j, rows(d)] + land[k, 2 + j].astype(F32) + land[k, 4 + j].astype(F32)

    def share(n, way, j):
        block = acts.at[n, j, rows(d)]
        recv = c_r.at[n, way] if way == j else f_r.at[n, j]
        remote(block, block, s_c, recv, x_dev[way])

    def relay(n, way):
        block = acts.at[n, way, rows((left, right)[way])]
        take(block, c_r.at[n, way])
        remote(block, block, s_c, f_r.at[n, way], x_dev[way])

    def shared(n, j):
        take(land.at[n, pl.ds(0, 2)], f_r.at[n, j])

    def forward_acts():
        for j in range(2):
            gate = total(0, j)
            up = total(1, j)
            sig = jax.nn.sigmoid(gate)
            active = gate * sig
            acts[0, j, rows(d)] = (active * up).astype(BF)
            share(0, j, j)
            share(0, 1 - j, j)
            keep[0, j] = up * (sig * (1.0 + gate * (1.0 - sig)))
            keep[1, j] = active

    def backward_acts():
        for j in range(2):
            back = total(2, j)
            acts[1, j, rows(d)] = (back * keep[0, j]).astype(BF)
            acts[2, j, rows(d)] = (back * keep[1, j]).astype(BF)
            if j == 0:
                share(1, 0, 0)
                share(2, 0, 0)
            share(1, 1, j)
            share(2, 1, j)

    def late_share():
        share(1, 0, 1)
        share(2, 0, 1)

    def rows_of(kd, j, columns):
        if kd == 0:
            return tn(acts[0, j], w[2, j, :, columns])
        return tn(acts[1, j], w[0, j, :, columns]) + tn(acts[2, j], w[1, j, :, columns])

    mine = pl.ds(pl.multiple_of(c * HALF, 16), HALF)
    theirs = pl.ds(pl.multiple_of(other * HALF, 16), HALF)
    counts = ((4, 3), (3, 4))

    def target(j, way, i):
        ahead = counts[j][way] - i
        return lax.rem(z + (ahead if way == 0 else NZ - ahead), NZ)

    def early(kd, j):
        for way in (0, 1):
            early_out[kd, j, way] = rows_of(kd, j, cols(target(j, way, 0)))
        remote(early_out.at[kd, j, :, theirs], early_in.at[kd, j], s_e, e_r.at[kd, j], sibling)

    def expand(kd, j):
        rows_out[kd, j] = rows_of(kd, j, slice(None))
        remote(rows_out.at[kd, j, theirs], twin_in.at[kd, j], s_t, t_r.at[kd, j], sibling)

    def chunk_sum(kd, j, q):
        return rows_out[kd, j, mine, cols(q)] + twin_in[kd, j, :, cols(q)]

    def ring_number(j, way, i):
        return i + (counts[j][0] if way else 0)

    def reduce_step(kd, j, i):
        if i == 0:
            take(early_in.at[kd, j], e_r.at[kd, j])
        if i == 1:
            take(twin_in.at[kd, j], t_r.at[kd, j])
        for way in (0, 1):
            if i >= counts[j][way]:
                continue
            number = ring_number(j, way, i)
            if i == 0:
                value = early_out[kd, j, way, mine] + early_in[kd, j, way]
            else:
                value = chunk_sum(kd, j, target(j, way, i))
                take(ring_in.at[kd, j, number - 1], r_r.at[kd, j, number - 1])
                value = value + ring_in[kd, j, number - 1].astype(F32)
            ring_out[kd, j, number] = value.astype(BF)
            remote(
                ring_out.at[kd, j, number], ring_in.at[kd, j, number],
                s_r, r_r.at[kd, j, number], (z_up, z_down)[way],
            )

    def go_home(kd, j):
        value = chunk_sum(kd, j, z)
        for way in (0, 1):
            number = ring_number(j, way, counts[j][way] - 1)
            take(ring_in.at[kd, j, number], r_r.at[kd, j, number])
            value = value + ring_in[kd, j, number].astype(F32)
        value = value.astype(BF)
        final[kd, j] = value
        home[kd, j, own(0, 1)] = value[:SHARE]
        for o in (2, 1, 3, 0):
            for same in (0, 1):
                if o == 0 and same == 0:
                    continue
                core = c if same == 0 else other
                remote(
                    final.at[kd, j, pl.ds(o * SHARE, SHARE)],
                    home.at[kd, j, own((NY - o) % NY, 1)],
                    s_h, h_r.at[kd],
                    {"expert": group[o], "tensor": z * 2 + core},
                )

    LANES = 2

    def band(n):
        size = TOK // 2 // LANES
        return pl.ds(pl.multiple_of(c * (TOK // 2) + n * size, size), size)

    outs = [
        [
            RingGather(
                lambda q, kd=kd, n=n: out.at[kd, band(n), cols(q)],
                z,
                z_up,
                z_down,
                sibling,
                (s_gz, gz_r.at[kd, n], s_gs, gs_r.at[kd]),
                *counts[n % 2],
            )
            for n in range(LANES)
        ]
        for kd in range(2)
    ]

    half = pl.ds(pl.multiple_of(c * (TOK // 2), TOK // 2), TOK // 2)
    other_half = pl.ds(pl.multiple_of(other * (TOK // 2), TOK // 2), TOK // 2)

    def settle(kd):
        take(ring_in.at[kd, :, :, pl.ds(0, SHARE)], h_r.at[kd])
        value = tn(slots[0, :, half], home[kd, 0]) + tn(slots[1, :, half], home[kd, 1])
        out[kd, half, cols(z)] = value.astype(BF)
        for lane in outs[kd]:
            lane.start()

    def circulate(kd, hop):
        for lane in outs[kd]:
            lane.step(hop)

    def weight_grad(n, k, j):
        wgrad[n, j] = nn(acts[n, j], x[k, j]).astype(BF)

    def finish(kd):
        take(out.at[kd, other_half], gs_r.at[kd])

    def drain():
        take(x.at[:, :, pl.ds(0, HALF), pl.ds(0, PART)], s_y)
        take(x.at[:, :, pl.ds(0, HALF - SHARE), pl.ds(0, PART)], s_z)
        take(x.at[:, :, pl.ds(0, HALF - SHARE)], s_w)
        take(land, s_b)
        take(land, s_c)
        take(twin_in, s_t)
        take(early_in, s_e)
        take(ring_in, s_r)
        take(ring_in.at[:, :, :, pl.ds(0, SHARE)], s_h)
        take(ring_in.at[:, :, :, pl.ds(0, TOK // 2 // LANES)], s_gz)
        take(out.at[:, half], s_gs)

    pick(0)
    pl.semaphore_wait(barrier, len(greet))
    launch_far(0)
    own_rows(0)
    pick(1)
    launch_near(0)
    pass_on(0)
    launch_far(1)
    spread(0, 3)
    spread(0, 1)
    launch_near(1)
    own_rows(1)
    spread(0, 2)
    pass_on(1)
    collect(0, 3)
    collect(0, 1)
    collect(0, 2)
    spread(1, 3)
    spread(1, 1)
    spread(1, 2)
    complete(0)
    loads[2].wait()
    partial(0)
    collect(1, 3)
    collect(1, 1)
    loads[3].wait()
    partial(1)
    collect(1, 2)
    join(0)
    complete(1)
    loads[4].wait()
    join(1)
    partial(2)
    arrived(0)
    arrived(1)
    forward_acts()
    join(2)
    relay(0, 0)
    relay(0, 1)
    arrived(2)
    backward_acts()
    shared(0, 0)
    shared(0, 1)
    early(0, 0)
    early(0, 1)
    expand(0, 0)
    expand(0, 1)
    reduce_step(0, 0, 0)
    reduce_step(0, 1, 0)
    relay(1, 0)
    weight_grad(0, 1, 0)
    relay(2, 0)
    late_share()
    weight_grad(0, 1, 1)
    reduce_step(0, 0, 1)
    reduce_step(0, 1, 1)
    relay(1, 1)
    relay(2, 1)
    shared(1, 0)
    shared(2, 0)
    early(1, 0)
    expand(1, 0)
    reduce_step(1, 0, 0)
    reduce_step(0, 0, 2)
    reduce_step(0, 1, 2)
    shared(1, 1)
    shared(2, 1)
    early(1, 1)
    expand(1, 1)
    reduce_step(1, 1, 0)
    reduce_step(1, 0, 1)
    reduce_step(0, 0, 3)
    reduce_step(0, 1, 3)
    weight_grad(1, 0, 0)
    reduce_step(1, 1, 1)
    reduce_step(1, 0, 2)
    weight_grad(1, 0, 1)
    go_home(0, 0)
    go_home(0, 1)
    reduce_step(1, 1, 2)
    reduce_step(1, 0, 3)
    weight_grad(2, 0, 0)
    settle(0)
    reduce_step(1, 1, 3)
    go_home(1, 0)
    weight_grad(2, 0, 1)
    circulate(0, 0)
    go_home(1, 1)
    circulate(0, 1)
    settle(1)
    circulate(0, 2)
    circulate(1, 0)
    circulate(0, 3)
    circulate(1, 1)
    circulate(1, 2)
    finish(0)
    circulate(1, 3)
    finish(1)
    drain()


def writer(out, wgrad, mix_hbm, gt_hbm, gg_hbm, gu_hbm, gd_hbm, sems):
    pairs = []
    for j in range(2):
        pairs.append((wgrad.at[1, j], gg_hbm.at[j]))
        pairs.append((wgrad.at[2, j], gu_hbm.at[j]))
        pairs.append((wgrad.at[0, j], gd_hbm.at[j]))
    pairs.append((out.at[0], mix_hbm))
    pairs.append((out.at[1], gt_hbm))
    copies = [pltpu.make_async_copy(a, b, sems.at[i]) for i, (a, b) in enumerate(pairs)]
    for copy in copies:
        copy.start()
    for copy in copies:
        copy.wait()


def body(tokens, labels, grad_out, w_gate, w_up, w_down):
    dma = pltpu.SemaphoreType.DMA
    scratch = [
        pltpu.VMEM((1, TOK), jnp.int32),
        pltpu.VMEM((2, TOK, FEAT), BF),
        pltpu.VMEM((3, 2, HID, FEAT), BF),
        pltpu.VMEM((2, ROWS, TOK), BF),
        pltpu.VMEM((2, 2, HALF - SHARE, PART), BF),
        pltpu.VMEM((2, 2, SHARE, PART), BF),
        pltpu.VMEM((2, 2, ROWS, FEAT), BF),
        pltpu.VMEM((3, 2, HID, ROWS), F32),
        pltpu.VMEM((3, 2, HID, ROWS), BF),
        pltpu.VMEM((3, 6, SLICE, ROWS), BF),
        pltpu.VMEM((3, 2, SLICE, ROWS), BF),
        pltpu.VMEM((3, 2, HID, ROWS), BF),
        pltpu.VMEM((2, 2, SLICE, ROWS), F32),
        pltpu.VMEM((2, 2, HALF, FEAT), F32),
        pltpu.VMEM((2, 2, 2, HALF, COL), F32),
        pltpu.VMEM((2, 2, 2, ROWS, COL), F32),
        pltpu.VMEM((2, 2, ROWS, FEAT), F32),
        pltpu.VMEM((2, 2, 7, HALF, COL), BF),
        pltpu.VMEM((2, 2, 7, HALF, COL), BF),
        pltpu.VMEM((2, 2, HALF, COL), BF),
        pltpu.VMEM((2, 2, ROWS, COL), BF),
        dma((6,)),
        dma((11,)),
        dma((2, 4)),
        dma((2, 3)),
        dma((2,)),
        dma((3, 2)),
        dma((3,)),
        dma((3, 2)),
        dma((3, 2)),
        dma((2, 2)),
        dma((2, 2)),
        dma((2, 2, 7)),
        dma((2,)),
        dma((2, 2, 7)),
        dma((2,)),
    ]
    hbm = pl.BlockSpec(memory_space=pltpu.HBM)
    vmem = pl.BlockSpec(memory_space=pltpu.VMEM)
    out, wgrad = pl.pallas_call(
        kernel,
        out_shape=(
            pltpu.VMEM((2, TOK, FEAT), BF),
            pltpu.VMEM((3, 2, HID, FEAT), BF),
        ),
        in_specs=[hbm] * 6,
        out_specs=(vmem, vmem),
        scratch_shapes=scratch,
        compiler_params=pltpu.CompilerParams(
            collective_id=0, has_side_effects=True, vmem_limit_bytes=50 * 1024 * 1024
        ),
    )(
        labels.reshape(1, TOK),
        tokens,
        grad_out,
        jnp.swapaxes(w_gate, 1, 2),
        jnp.swapaxes(w_up, 1, 2),
        w_down,
    )
    out = pltpu.with_memory_space_constraint(out, pltpu.VMEM)
    wgrad = pltpu.with_memory_space_constraint(wgrad, pltpu.VMEM)
    weights = jax.ShapeDtypeStruct((2, HID, FEAT), BF)
    acts = jax.ShapeDtypeStruct((TOK, FEAT), BF)
    mixed, grad_tokens, gate_t, up_t, down = pl.pallas_call(
        writer,
        out_shape=(acts, acts, weights, weights, weights),
        in_specs=[vmem, vmem],
        out_specs=(hbm,) * 5,
        scratch_shapes=[dma((8,))],
        compiler_params=pltpu.CompilerParams(vmem_limit_bytes=4 * 1024 * 1024),
    )(out, wgrad)
    return mixed, grad_tokens, jnp.swapaxes(gate_t, 1, 2), jnp.swapaxes(up_t, 1, 2), down


def solution(mesh):
    in_specs = (
        P("expert", "dp"),
        P("expert", None),
        P("expert", "dp"),
        P("expert", "dp", "tensor"),
        P("expert", "dp", "tensor"),
        P("expert", "tensor", "dp"),
    )
    out_specs = (
        P("expert", "dp"),
        P("expert", "dp"),
        P("expert", "dp", "tensor"),
        P("expert", "dp", "tensor"),
        P("expert", "tensor", "dp"),
    )
    return jax.shard_map(body, mesh=mesh, in_specs=in_specs, out_specs=out_specs, check_vma=False)
```

time: 313 us -> 102 us (0.33)
  blocking collectives: 203 us -> 0 us
  Pallas kernels: 0 us -> 101 us
  local copies, waits for them, and re-layouts: 40.4 us -> 0 us
  waiting for transfers between devices: 26.3 us -> 0 us
  matrix products: 25.8 us -> 0 us
  other arithmetic: 9.35 us -> 0 us
  starting transfers between devices: 4.77 us -> 0 us
    all_to_all x3 -> x0, blocking collectives: 119 us -> none  [the longest x1 51.8 us: summed_on_arrival(): tiles = lax.all_to_all(split_up(shard, dim, count), axis, 0, 0, tiled=True)]
    pallas_call x0 -> x2, Pallas kernels: none -> 101 us  [the longest x1 98.1 us: body(): pl.pallas_call(kernel, out_shape=(pltpu.VMEM((2, TOK, FEAT), BF), pltpu.V...]
    psum x1 -> x0, blocking collectives: 83.2 us -> none  [body(): summed = lax.psum(rows_out, 'tensor').astype(jnp.bfloat16)]
    all_to_all x1 -> x0, waiting for transfers between devices: 26.3 us -> none  [body(): lax.all_to_all(summed, 'expert', split_axis=1, concat_axis=1, tiled=True)]
    dot_general x11 -> x0, matrix products: 25.8 us -> none  [the longest x1 4.99 us: body(): jnp.dot(to_slots, payload, preferred_element_type=jnp.float32)]
    reshape x4 -> x0, local copies, waits for them, and re-layouts: 17.9 us -> none  [the longest x2 9.61 us: body(): packed = packed.reshape(MOST, groups, local_experts, 2 * feat_width)]
    all_to_all x2 -> x0, local copies, waits for them, and re-layouts: 7.01 us -> none  [the longest x1 6.84 us: body(): lax.all_to_all(summed, 'expert', split_axis=1, concat_axis=1, tiled=True)]
    concatenate x2 -> x0, local copies, waits for them, and re-layouts: 5.9 us -> none  [the longest x1 5.54 us: body(): jnp.concatenate([gate_part, up_part, back_part], axis=-1)]
  transfers between devices with their start and end apart: 1 -> 0, of which waited for: 1 -> 0; matrix products, arithmetic and copies ran while one was open for 3% -> 0% of each run, Pallas kernels for 0% -> 0%
where the time goes in v2:
time: 102 us
  Pallas kernels  101 us (99%)
    pallas_call x1, Pallas kernels, body(): pl.pallas_call(kernel, out_shape=(pltpu.VMEM((2, TOK, FEAT), BF), pltpu.V...  98.1 us
    pallas_call x1, Pallas kernels, body(): pl.pallas_call(writer, out_shape=(acts, acts, weights, weights, weights),...  3.14 us

profile of v2, /device:TPU:1, one launch (start us, length us, event | category | flops | bytes accessed | tf_op | source)
XLA Modules:
  0.0 101.9 jit_solution(6871342166626408575)
XLA Ops:
  0.6 98.1 %shard_map.101 = (bf16[2,512,1024]{2,1,0:T(8,128)(2,1)S(1)}, bf16[3,2,448,1024]{3,2,1,0:T(8,128)(2,1)S(1)}) custom-call(s32[1,512]{1,0:T(1,128)} %bitcast.7, bf16[512,1024]{1,0:T(8,128)(2,1)} %tok_hbm.1, bf16[512,1024]{1,0:T(8,128)(2,1)} %go_hbm.1, bf16[2,448,1024]{2,1,0:T(8,128)(2,1)} %bitcast.5, bf16[2,448,1024]{2,1,0:T(8,128)(2,1)} %bitcast.6, ...), custom_call_target="tpu_custom_call" | custom-call | tf_op jit(solution)/shard_map/pallas_call | solution.py:598
  98.7 3.1 %shard_map.102 = (bf16[512,1024]{1,0:T(8,128)(2,1)}, bf16[512,1024]{1,0:T(8,128)(2,1)}, bf16[2,448,1024]{2,1,0:T(8,128)(2,1)}, bf16[2,448,1024]{2,1,0:T(8,128)(2,1)}, bf16[2,448,1024]{2,1,0:T(8,128)(2,1)}) custom-call(bf16[2,512,1024]{2,1,0:T(8,128)(2,1)S(1)} %get-tuple-element.12.out, bf16[3,2,448,1024]{3,2,1,0:T(8,128)(2,1)S(1)} %get-tuple-element.13.wgrad), custom_call_target="tpu_custom_call" | custom-call | tf_op jit(solution)/shard_map/pallas_call | solution.py:622

commit v3 on v2

--- a/solution.py
+++ b/solution.py
@@ -194,9 +194,18 @@
         start = parity * PART + way * (PART // 2)
         return pl.ds(pl.multiple_of(start, PART // 2), PART // 2)
 
-    def pick(k):
-        loads[k].wait()
-        for j in range(2):
+    parcels = ((0, 0, 1), (0, 1, 1), (1, 0, 2))
+    present = set()
+
+    def loaded(number):
+        if number not in present:
+            present.add(number)
+            loads[number].wait()
+
+    def pick(p):
+        k, first, count = parcels[p]
+        loaded(k)
+        for j in range(first, first + count):
             outgo[k, j] = nn(slots[j, own(1, NY - 1)], src[k, :, span]).astype(BF)
 
     def remote(source, target, send, recv, device):
@@ -205,112 +214,127 @@
     onward = {"expert": lax.rem(g + 1 + 2 * c, NY)}
     other_span = pl.ds(pl.multiple_of(PART - lax.rem(z, 2) * PART, PART), PART)
 
-    def launch_far(k):
-        remote(outgo.at[k, :, pl.ds(SHARE, SHARE)], passing.at[k], s_y, y_r.at[k, 2], onward)
-
-    def launch_near(k):
+    def outgoing(p, o):
+        k, first, count = parcels[p]
+        return outgo.at[k, pl.ds(first, count), pl.ds((o - 1) * SHARE, SHARE)]
+
+    def passage(p):
+        k, first, count = parcels[p]
+        return passing.at[k, pl.ds(first, count)]
+
+    def landed(p, block, columns):
+        k, first, count = parcels[p]
+        return x.at[k, pl.ds(first, count), own(block, 1), columns]
+
+    def launch_far(p):
+        remote(outgoing(p, 2), passage(p), s_y, y_r.at[p, 2], onward)
+
+    def launch_near(p):
         for o in (1, 3):
             remote(
-                outgo.at[k, :, pl.ds((o - 1) * SHARE, SHARE)],
-                x.at[k, :, own(NY - o, 1), span],
-                s_y, y_r.at[k, NY - o], {"expert": group[o]},
+                outgoing(p, o), landed(p, NY - o, span), s_y, y_r.at[p, NY - o], {"expert": group[o]}
             )
 
-    def pass_on(k):
-        take(passing.at[k], y_r.at[k, 2])
-        remote(passing.at[k], x.at[k, :, own(2, 1), span], s_y, y_r.at[k, 0], onward)
+    def pass_on(p):
+        take(passage(p), y_r.at[p, 2])
+        remote(passage(p), landed(p, 2, span), s_y, y_r.at[p, 0], onward)
 
     def own_rows(k):
+        loaded(k)
         for j in range(2):
             both = jnp.concatenate([slots[j, pl.ds(0, SHARE)], slots[j, pl.ds(HALF, SHARE)]], axis=0)
             value = nn(both, src[k]).astype(BF)
             x[k, j, pl.ds(0, SHARE)] = value[:SHARE]
             x[k, j, pl.ds(HALF, SHARE)] = value[SHARE:]
 
-    def twin(k, block, columns):
-        part_ref = x.at[k, :, own(block, 1), columns]
-        remote(part_ref, part_ref, s_w, w_r.at[k], sibling)
-
-    def spread(k, block):
-        take(x.at[k, :, own(block, 1), span], y_r.at[k, 0 if block == 2 else block])
+    def twin(p, block, columns):
+        remote(landed(p, block, columns), landed(p, block, columns), s_w, w_r.at[p], sibling)
+
+    def spread(p, block):
+        take(landed(p, block, span), y_r.at[p, 0 if block == 2 else block])
         for way in (0, 1):
-            part_ref = x.at[k, :, own(block, 1), quarter(lax.rem(z, 2), way)]
-            remote(part_ref, part_ref, s_z, z_r.at[k, block - 1], (z_up, z_down)[way])
-        twin(k, block, span)
-
-    def collect(k, block):
-        take(x.at[k, :, own(block, 1), other_span], z_r.at[k, block - 1])
-        twin(k, block, other_span)
-
-    def complete(k):
+            part_ref = landed(p, block, quarter(lax.rem(z, 2), way))
+            remote(part_ref, part_ref, s_z, z_r.at[p, block - 1], (z_up, z_down)[way])
+        twin(p, block, span)
+
+    def collect(p, block):
+        take(landed(p, block, other_span), z_r.at[p, block - 1])
+        twin(p, block, other_span)
+
+    def complete(p):
+        k, first, count = parcels[p]
         theirs_x = pl.ds(pl.multiple_of(other * HALF + SHARE, 16), HALF - SHARE)
-        take(x.at[k, :, theirs_x], w_r.at[k])
-
-    def partial(k):
-        for j in range(2):
-            value = nt(w[k, j], x[1 if k == 2 else 0, j])
-            part[k, j] = value
-            part16[k, j] = value.astype(BF)
-            way = j
-            remote(part16.at[k, j, rows(far)], land.at[k, way], s_b, v_r.at[k, way], x_dev[way])
-            way = 1 - j
-            remote(
-                part16.at[k, j, rows((right, left)[way])], land.at[k, 2 + 2 * way + j],
-                s_b, b_r.at[k], x_dev[way],
-            )
-
-    def join(k):
-        for way in (0, 1):
-            take(land.at[k, way], v_r.at[k, way])
-            near = rows((right, left)[way])
-            joined[k, way] = (part[k, way, near] + land[k, way].astype(F32)).astype(BF)
-            remote(joined.at[k, way], land.at[k, 2 + 2 * way + way], s_b, b_r.at[k], x_dev[way])
-
-    def arrived(k):
-        take(land.at[k, pl.ds(2, 4)], b_r.at[k])
+        take(x.at[k, pl.ds(first, count), theirs_x], w_r.at[p])
+
+    def way_in(k, j):
+        return j ^ (k & 1)
+
+    def way_out(n, j):
+        return (1 - j, j, 1 - j)[n]
+
+    sides = (right, left)
+
+    def partial(k, j):
+        loaded(2 + k)
+        value = nt(w[k, j], x[1 if k == 2 else 0, j])
+        part[k, j] = value
+        part16[k, j] = value.astype(BF)
+        way = way_in(k, j)
+        remote(part16.at[k, j, rows(far)], land.at[k, j, 0], s_b, v_r.at[k, j], x_dev[way])
+        way = 1 - way
+        remote(
+            part16.at[k, j, rows(sides[way])], land.at[k, j, 1], s_b, b_r.at[k, j], x_dev[way]
+        )
+
+    def join(k, j):
+        take(land.at[k, j, 0], v_r.at[k, j])
+        way = way_in(k, j)
+        joined[k, j] = (part[k, j, rows(sides[way])] + land[k, j, 0].astype(F32)).astype(BF)
+        remote(joined.at[k, j], land.at[k, j, 2], s_b, b_r.at[k, j], x_dev[way])
 
     def total(k, j):
-        return part[k, j, rows(d)] + land[k, 2 + j].astype(F32) + land[k, 4 + j].astype(F32)
-
-    def share(n, way, j):
+        take(land.at[k, j, pl.ds(1, 2)], b_r.at[k, j])
+        return part[k, j, rows(d)] + land[k, j, 1].astype(F32) + land[k, j, 2].astype(F32)
+
+    def share(n, j, direct):
         block = acts.at[n, j, rows(d)]
-        recv = c_r.at[n, way] if way == j else f_r.at[n, j]
-        remote(block, block, s_c, recv, x_dev[way])
-
-    def relay(n, way):
-        block = acts.at[n, way, rows((left, right)[way])]
-        take(block, c_r.at[n, way])
-        remote(block, block, s_c, f_r.at[n, way], x_dev[way])
+        way = way_out(n, j)
+        if direct:
+            remote(block, block, s_c, f_r.at[n, j], x_dev[1 - way])
+        else:
+            remote(block, block, s_c, c_r.at[n, j], x_dev[way])
+
+    def relay(n, j):
+        way = way_out(n, j)
+        block = acts.at[n, j, rows((left, right)[way])]
+        take(block, c_r.at[n, j])
+        remote(block, block, s_c, f_r.at[n, j], x_dev[way])
+
+    gathered = set()
 
     def shared(n, j):
-        take(land.at[n, pl.ds(0, 2)], f_r.at[n, j])
-
-    def forward_acts():
-        for j in range(2):
-            gate = total(0, j)
-            up = total(1, j)
-            sig = jax.nn.sigmoid(gate)
-            active = gate * sig
-            acts[0, j, rows(d)] = (active * up).astype(BF)
-            share(0, j, j)
-            share(0, 1 - j, j)
-            keep[0, j] = up * (sig * (1.0 + gate * (1.0 - sig)))
-            keep[1, j] = active
-
-    def backward_acts():
-        for j in range(2):
-            back = total(2, j)
-            acts[1, j, rows(d)] = (back * keep[0, j]).astype(BF)
-            acts[2, j, rows(d)] = (back * keep[1, j]).astype(BF)
-            if j == 0:
-                share(1, 0, 0)
-                share(2, 0, 0)
-            share(1, 1, j)
-            share(2, 1, j)
-
-    def late_share():
-        share(1, 0, 1)
-        share(2, 0, 1)
+        if (n, j) not in gathered:
+            gathered.add((n, j))
+            take(land.at[n, 0, pl.ds(0, 2)], f_r.at[n, j])
+
+    def forward_acts(j):
+        gate = total(0, j)
+        up = total(1, j)
+        sig = jax.nn.sigmoid(gate)
+        active = gate * sig
+        acts[0, j, rows(d)] = (active * up).astype(BF)
+        share(0, j, False)
+        share(0, j, True)
+        keep[0, j] = up * (sig * (1.0 + gate * (1.0 - sig)))
+        keep[1, j] = active
+
+    def backward_acts(j):
+        back = total(2, j)
+        acts[1, j, rows(d)] = (back * keep[0, j]).astype(BF)
+        acts[2, j, rows(d)] = (back * keep[1, j]).astype(BF)
+        for direct in (False, True):
+            share(1, j, direct)
+            share(2, j, direct)
 
     def rows_of(kd, j, columns):
         if kd == 0:
@@ -325,12 +349,18 @@
         ahead = counts[j][way] - i
         return lax.rem(z + (ahead if way == 0 else NZ - ahead), NZ)
 
+    def ready(kd, j):
+        for n in ((0,), (1, 2))[kd]:
+            shared(n, j)
+
     def early(kd, j):
+        ready(kd, j)
         for way in (0, 1):
             early_out[kd, j, way] = rows_of(kd, j, cols(target(j, way, 0)))
         remote(early_out.at[kd, j, :, theirs], early_in.at[kd, j], s_e, e_r.at[kd, j], sibling)
 
     def expand(kd, j):
+        ready(kd, j)
         rows_out[kd, j] = rows_of(kd, j, slice(None))
         remote(rows_out.at[kd, j, theirs], twin_in.at[kd, j], s_t, t_r.at[kd, j], sibling)
 
@@ -419,6 +449,7 @@
             lane.step(hop)
 
     def weight_grad(n, k, j):
+        shared(n, j)
         wgrad[n, j] = nn(acts[n, j], x[k, j]).astype(BF)
 
     def finish(kd):
@@ -437,102 +468,108 @@
         take(ring_in.at[:, :, :, pl.ds(0, TOK // 2 // LANES)], s_gz)
         take(out.at[:, half], s_gs)
 
+    pick(1)
+    pl.semaphore_wait(barrier, len(greet))
+    launch_far(1)
+    launch_near(1)
     pick(0)
-    pl.semaphore_wait(barrier, len(greet))
     launch_far(0)
+    pass_on(1)
+    launch_near(0)
+    spread(1, 1)
+    spread(1, 3)
+    pass_on(0)
+    pick(2)
+    launch_far(2)
+    launch_near(2)
+    spread(1, 2)
+    collect(1, 1)
+    spread(0, 3)
+    collect(1, 3)
     own_rows(0)
-    pick(1)
-    launch_near(0)
-    pass_on(0)
-    launch_far(1)
-    spread(0, 3)
     spread(0, 1)
-    launch_near(1)
-    own_rows(1)
+    collect(1, 2)
     spread(0, 2)
-    pass_on(1)
+    complete(1)
+    partial(0, 1)
+    pass_on(2)
     collect(0, 3)
     collect(0, 1)
+    partial(1, 1)
     collect(0, 2)
-    spread(1, 3)
-    spread(1, 1)
-    spread(1, 2)
+    spread(2, 3)
     complete(0)
-    loads[2].wait()
-    partial(0)
-    collect(1, 3)
-    collect(1, 1)
-    loads[3].wait()
-    partial(1)
-    collect(1, 2)
-    join(0)
-    complete(1)
-    loads[4].wait()
-    join(1)
-    partial(2)
-    arrived(0)
-    arrived(1)
-    forward_acts()
-    join(2)
+    spread(2, 1)
+    partial(0, 0)
+    partial(1, 0)
+    own_rows(1)
+    spread(2, 2)
+    join(1, 1)
+    collect(2, 1)
+    join(0, 1)
+    join(0, 0)
+    collect(2, 3)
+    collect(2, 2)
+    join(1, 0)
+    complete(2)
+    partial(2, 1)
+    forward_acts(1)
+    forward_acts(0)
+    join(2, 1)
+    partial(2, 0)
+    relay(0, 1)
     relay(0, 0)
-    relay(0, 1)
-    arrived(2)
-    backward_acts()
-    shared(0, 0)
-    shared(0, 1)
+    join(2, 0)
+    backward_acts(1)
+    backward_acts(0)
     early(0, 0)
     early(0, 1)
-    expand(0, 0)
-    expand(0, 1)
+    relay(1, 1)
+    relay(2, 1)
     reduce_step(0, 0, 0)
     reduce_step(0, 1, 0)
+    expand(0, 1)
+    expand(0, 0)
     relay(1, 0)
-    weight_grad(0, 1, 0)
-    relay(2, 0)
-    late_share()
-    weight_grad(0, 1, 1)
     reduce_step(0, 0, 1)
     reduce_step(0, 1, 1)
-    relay(1, 1)
-    relay(2, 1)
-    shared(1, 0)
-    shared(2, 0)
+    relay(2, 0)
+    weight_grad(0, 1, 0)
+    early(1, 1)
+    reduce_step(0, 0, 2)
     early(1, 0)
+    reduce_step(1, 1, 0)
+    expand(1, 1)
+    reduce_step(1, 0, 0)
     expand(1, 0)
-    reduce_step(1, 0, 0)
-    reduce_step(0, 0, 2)
     reduce_step(0, 1, 2)
-    shared(1, 1)
-    shared(2, 1)
-    early(1, 1)
-    expand(1, 1)
-    reduce_step(1, 1, 0)
+    reduce_step(1, 1, 1)
     reduce_step(1, 0, 1)
+    reduce_step(0, 1, 3)
     reduce_step(0, 0, 3)
-    reduce_step(0, 1, 3)
-    weight_grad(1, 0, 0)
-    reduce_step(1, 1, 1)
+    reduce_step(1, 1, 2)
+    weight_grad(2, 0, 0)
     reduce_step(1, 0, 2)
+    go_home(0, 1)
     weight_grad(1, 0, 1)
     go_home(0, 0)
-    go_home(0, 1)
-    reduce_step(1, 1, 2)
+    reduce_step(1, 1, 3)
     reduce_step(1, 0, 3)
-    weight_grad(2, 0, 0)
     settle(0)
-    reduce_step(1, 1, 3)
+    go_home(1, 1)
     go_home(1, 0)
+    weight_grad(0, 1, 1)
+    circulate(0, 0)
+    settle(1)
+    circulate(0, 1)
+    circulate(1, 0)
+    circulate(0, 2)
+    circulate(1, 1)
+    circulate(0, 3)
+    circulate(1, 2)
+    weight_grad(1, 0, 0)
+    finish(0)
     weight_grad(2, 0, 1)
-    circulate(0, 0)
-    go_home(1, 1)
-    circulate(0, 1)
-    settle(1)
-    circulate(0, 2)
-    circulate(1, 0)
-    circulate(0, 3)
-    circulate(1, 1)
-    circulate(1, 2)
-    finish(0)
     circulate(1, 3)
     finish(1)
     drain()
@@ -565,7 +602,7 @@
         pltpu.VMEM((2, 2, ROWS, FEAT), BF),
         pltpu.VMEM((3, 2, HID, ROWS), F32),
         pltpu.VMEM((3, 2, HID, ROWS), BF),
-        pltpu.VMEM((3, 6, SLICE, ROWS), BF),
+        pltpu.VMEM((3, 2, 3, SLICE, ROWS), BF),
         pltpu.VMEM((3, 2, SLICE, ROWS), BF),
         pltpu.VMEM((3, 2, HID, ROWS), BF),
         pltpu.VMEM((2, 2, SLICE, ROWS), F32),
@@ -579,11 +616,11 @@
         pltpu.VMEM((2, 2, ROWS, COL), BF),
         dma((6,)),
         dma((11,)),
-        dma((2, 4)),
-        dma((2, 3)),
-        dma((2,)),
+        dma((3, 4)),
+        dma((3, 3)),
+        dma((3,)),
         dma((3, 2)),
-        dma((3,)),
+        dma((3, 2)),
         dma((3, 2)),
         dma((3, 2)),
         dma((2, 2)),

time: 102 us -> 96.8 us (0.949)
  Pallas kernels: 101 us -> 96.1 us
    pallas_call x1, Pallas kernels: 98.1 us -> 92.9 us  [body(): pl.pallas_call(kernel, out_shape=(pltpu.VMEM((2, TOK, FEAT), BF), pltpu.V...]
where the time goes in v3:
time: 96.8 us; the launch traced here: 96.7 us
  Pallas kernels  96.1 us (99%)
    pallas_call x1, Pallas kernels, body(): pl.pallas_call(kernel, out_shape=(pltpu.VMEM((2, TOK, FEAT), BF), pltpu.V...  92.9 us
    pallas_call x1, Pallas kernels, body(): pl.pallas_call(writer, out_shape=(acts, acts, weights, weights, weights),...  3.14 us

profile of v3, /device:TPU:1, one launch (start us, length us, event | category | flops | bytes accessed | tf_op | source)
XLA Modules:
  0.0 96.7 jit_solution(14997500354170654568)
XLA Ops:
  0.6 92.9 %shard_map.101 = (bf16[2,512,1024]{2,1,0:T(8,128)(2,1)S(1)}, bf16[3,2,448,1024]{3,2,1,0:T(8,128)(2,1)S(1)}) custom-call(s32[1,512]{1,0:T(1,128)} %bitcast.7, bf16[512,1024]{1,0:T(8,128)(2,1)} %tok_hbm.1, bf16[512,1024]{1,0:T(8,128)(2,1)} %go_hbm.1, bf16[2,448,1024]{2,1,0:T(8,128)(2,1)} %bitcast.5, bf16[2,448,1024]{2,1,0:T(8,128)(2,1)} %bitcast.6, ...), custom_call_target="tpu_custom_call" | custom-call | tf_op jit(solution)/shard_map/pallas_call | solution.py:635
  93.6 3.1 %shard_map.102 = (bf16[512,1024]{1,0:T(8,128)(2,1)}, bf16[512,1024]{1,0:T(8,128)(2,1)}, bf16[2,448,1024]{2,1,0:T(8,128)(2,1)}, bf16[2,448,1024]{2,1,0:T(8,128)(2,1)}, bf16[2,448,1024]{2,1,0:T(8,128)(2,1)}) custom-call(bf16[2,512,1024]{2,1,0:T(8,128)(2,1)S(1)} %get-tuple-element.12.out, bf16[3,2,448,1024]{3,2,1,0:T(8,128)(2,1)S(1)} %get-tuple-element.13.wgrad), custom_call_target="tpu_custom_call" | custom-call | tf_op jit(solution)/shard_map/pallas_call | solution.py:659

commit v4 on v3

--- a/solution.py
+++ b/solution.py
@@ -94,6 +94,7 @@
     x,
     part,
     part16,
+    ahead,
     land,
     joined,
     acts,
@@ -273,14 +274,21 @@
         return (1 - j, j, 1 - j)[n]
 
     sides = (right, left)
+    begun = []
 
     def partial(k, j):
         loaded(2 + k)
+        way = way_in(k, j)
+        first = not begun
+        if first:
+            begun.append((k, j))
+            ahead[...] = nt(w[k, j, rows(far)], x[0, j]).astype(BF)
+            remote(ahead, land.at[k, j, 0], s_b, v_r.at[k, j], x_dev[way])
         value = nt(w[k, j], x[1 if k == 2 else 0, j])
         part[k, j] = value
         part16[k, j] = value.astype(BF)
-        way = way_in(k, j)
-        remote(part16.at[k, j, rows(far)], land.at[k, j, 0], s_b, v_r.at[k, j], x_dev[way])
+        if not first:
+            remote(part16.at[k, j, rows(far)], land.at[k, j, 0], s_b, v_r.at[k, j], x_dev[way])
         way = 1 - way
         remote(
             part16.at[k, j, rows(sides[way])], land.at[k, j, 1], s_b, b_r.at[k, j], x_dev[way]
@@ -602,6 +610,7 @@
         pltpu.VMEM((2, 2, ROWS, FEAT), BF),
         pltpu.VMEM((3, 2, HID, ROWS), F32),
         pltpu.VMEM((3, 2, HID, ROWS), BF),
+        pltpu.VMEM((SLICE, ROWS), BF),
         pltpu.VMEM((3, 2, 3, SLICE, ROWS), BF),
         pltpu.VMEM((3, 2, SLICE, ROWS), BF),
         pltpu.VMEM((3, 2, HID, ROWS), BF),

time: 96.8 us -> 97 us (level)
  no operation moved by 1% of the time
where the time goes in v4:
time: 97 us; the launch traced here: 96.9 us
  Pallas kernels  96.3 us (99%)
    pallas_call x1, Pallas kernels, body(): pl.pallas_call(kernel, out_shape=(pltpu.VMEM((2, TOK, FEAT), BF), pltpu.V...  93.2 us
    pallas_call x1, Pallas kernels, body(): pl.pallas_call(writer, out_shape=(acts, acts, weights, weights, weights),...  3.14 us

profile of v4, /device:TPU:1, one launch (start us, length us, event | category | flops | bytes accessed | tf_op | source)
XLA Modules:
  0.0 96.9 jit_solution(10028475572467159436)
XLA Ops:
  0.6 93.2 %shard_map.101 = (bf16[2,512,1024]{2,1,0:T(8,128)(2,1)S(1)}, bf16[3,2,448,1024]{3,2,1,0:T(8,128)(2,1)S(1)}) custom-call(s32[1,512]{1,0:T(1,128)} %bitcast.7, bf16[512,1024]{1,0:T(8,128)(2,1)} %tok_hbm.1, bf16[512,1024]{1,0:T(8,128)(2,1)} %go_hbm.1, bf16[2,448,1024]{2,1,0:T(8,128)(2,1)} %bitcast.5, bf16[2,448,1024]{2,1,0:T(8,128)(2,1)} %bitcast.6, ...), custom_call_target="tpu_custom_call" | custom-call | tf_op jit(solution)/shard_map/pallas_call | solution.py:644
  93.8 3.1 %shard_map.102 = (bf16[512,1024]{1,0:T(8,128)(2,1)}, bf16[512,1024]{1,0:T(8,128)(2,1)}, bf16[2,448,1024]{2,1,0:T(8,128)(2,1)}, bf16[2,448,1024]{2,1,0:T(8,128)(2,1)}, bf16[2,448,1024]{2,1,0:T(8,128)(2,1)}) custom-call(bf16[2,512,1024]{2,1,0:T(8,128)(2,1)S(1)} %get-tuple-element.12.out, bf16[3,2,448,1024]{3,2,1,0:T(8,128)(2,1)S(1)} %get-tuple-element.13.wgrad), custom_call_target="tpu_custom_call" | custom-call | tf_op jit(solution)/shard_map/pallas_call | solution.py:668
